TPU v7x, 256 devices: a whole 4x4x8 slice. The times are simulated.
256 devices in a mesh: seq: 64 (over y, x, z_hi, core), chan: 4 (over z_lo).
Axes of the slice: x: 4, y: 4, z: 8 (z_hi: 2, z_lo: 4; z = z_hi * 4 + z_lo), core: 2. Of those that a mesh axis runs over, the one named last changes fastest.
Arguments:
- tokens: bfloat16 [512, 768, 1024], P('seq', 'chan'), may hold values from -24 to 24, as said below
- filter_gain: bfloat16 [512, 768, 1024], P('seq', 'chan'), may hold values from -4 to 4
- row_factor: bfloat16 [1024, 1024], replicated, may hold values from -0.1875 to 0.1875
- col_factor: bfloat16 [512, 512], replicated, may hold values from -0.25 to 0.25
- up_weight: bfloat16 [4, 192, 768], P('chan'), may hold values from -0.4375 to 0.4375
- down_weight: bfloat16 [4, 192, 768], P('chan'), may hold values from -0.21875 to 0.21875
Outputs:
- layer_out: bfloat16 [512, 768, 1024], P('seq', 'chan')
Inputs may be any that keep to these rules, and one draw needn't show every extreme that they name: `tokens`: layer activations.
All inputs are finite; a program needn't handle non-finite values.
Results may differ from a plain program's by a relative error of at most 0.0075.
Values may be sent and summed in bfloat16 or wider, within the bound.
A program may use at most 128 MiB of HBM per device.

v0:
```python
import jax
import jax.numpy as jnp
from jax import lax
from jax.sharding import PartitionSpec as P

D = 768


def finish(source, mixed, up_weight, down_weight):
    src = source.astype(jnp.float32)
    gated = src + mixed.astype(jnp.float32) * jax.nn.sigmoid(src)
    total = lax.psum(jnp.sum(gated, axis=1), "chan")
    mean = total / D
    centered = gated - mean[:, None, :]
    spread = lax.psum(jnp.sum(centered * centered, axis=1), "chan") / D
    normed = (centered * lax.rsqrt(spread + 1e-05)[:, None, :]).astype(jnp.bfloat16)
    hidden = jax.nn.gelu(
        jnp.einsum("xky,kh->xhy", normed, up_weight[0], preferred_element_type=jnp.float32)
    ).astype(jnp.bfloat16)
    back = jnp.einsum("xhy,kh->xky", hidden, down_weight[0], preferred_element_type=jnp.float32)
    return (gated + back).astype(jnp.bfloat16)


def body(tokens, filter_gain, row_factor, col_factor, up_weight, down_weight):
    spun = jnp.einsum("rck,bk->rcb", tokens, row_factor, preferred_element_type=jnp.float32)
    filtered = (filter_gain.astype(jnp.float32) * spun).astype(jnp.bfloat16)
    by_channel = jnp.transpose(filtered, (1, 0, 2))
    owned = lax.all_to_all(by_channel, "seq", split_axis=0, concat_axis=1, tiled=True)
    mixed = jnp.einsum("ak,ckb->cab", col_factor, owned, preferred_element_type=jnp.float32)
    back = lax.all_to_all(
        mixed.astype(jnp.bfloat16), "seq", split_axis=1, concat_axis=0, tiled=True
    )
    return finish(tokens, jnp.transpose(back, (1, 0, 2)), up_weight, down_weight)


def solution(mesh):
    return jax.shard_map(
        body,
        mesh=mesh,
        in_specs=(
            P("seq", "chan", None),
            P("seq", "chan", None),
            P(),
            P(),
            P("chan", None, None),
            P("chan", None, None),
        ),
        out_specs=P("seq", "chan", None),
        check_vma=False,
    )
```

profile of v0, /device:TPU:2, one launch (start us, length us, event | category | flops | bytes accessed | tf_op | source)
XLA Modules:
  0.0 280.5 jit_solution(5488151017067106785)
XLA Ops:
  0.0 0.0 copy-start
  0.0 1.6 copy-done
  1.6 6.1 %fusion.17 = bf16[192,8,1024]{2,0,1:T(8,128)(2,1)S(1)} fusion(bf16[8,192,1024]{2,1,0:T(8,128)(2,1)} %param.7, bf16[8,192,1024]{2,1,0:T(8,128)(2,1)} %param.6, bf16[1024,1024]{1,0:T(8,128)(2,1)S(1)} %copy-done), kind=kOutput, calls=%fused_computation.23 | convolution fusion | flops 3225944064 | bytes 11534336 | tf_op jit(solution)/shard_map/rck,bk->rcb/dot_general | solution.py:25
  7.7 0.0 copy-start.2
  7.7 1.7 copy.17
  9.4 91.3 %all_to_all.27 = bf16[192,8,1024]{2,1,0:T(8,128)(2,1)S(1)} all-to-all(bf16[192,8,1024]{2,1,0:T(8,128)(2,1)S(1)} %copy.17), channel_id=1, replica_groups=mesh['seq'=64,'chan'=4] {'seq'}, dimensions={0} | all-to-all | bytes 6291456 | tf_op jit(solution)/shard_map/all_to_all | solution.py:28
  100.7 0.0 copy-done.2
  100.7 3.5 %convert_bitcast_fusion.1 = bf16[3,512,1024]{1,2,0:T(8,128)(2,1)} fusion(bf16[3,64,8,1024]{3,2,0,1:T(8,128)(2,1)S(1)} %bitcast.47, bf16[512,512]{1,0:T(8,128)(2,1)S(1)} %copy-done.2), kind=kOutput, calls=%fused_computation.29 | convolution fusion | flops 1612185600 | bytes 6815744 | tf_op jit(solution)/shard_map/ak,ckb->cab/dot_general | solution.py:29
  104.2 7.8 %copy.20 = bf16[3,512,1024]{2,0,1:T(4,128)(2,1)} copy(bf16[3,512,1024]{1,2,0:T(8,128)(2,1)} %convert_bitcast_fusion.1) | data formatting | bytes 6291456 | tf_op jit(solution)/shard_map/convert_element_type | solution.py:31
  112.0 71.4 %all_to_all.28 = bf16[3,512,1024]{2,0,1:T(4,128)(2,1)S(1)} all-to-all(bf16[3,512,1024]{2,0,1:T(4,128)(2,1)} %copy.20), channel_id=1, replica_groups=mesh['seq'=64,'chan'=4] {'seq'}, dimensions={1} | all-to-all | bytes 6291456 | tf_op jit(solution)/shard_map/all_to_all | solution.py:30
  183.4 1.4 convert_bitcast_fusion
  184.7 0.0 copy-start.1
  184.7 1.1 copy.22
  185.9 0.8 copy-done.1
  186.6 8.3 %fusion.38 = (f32[8,1024]{1,0:T(8,128)S(1)}, f32[8,192,1024]{2,1,0:T(8,128)}) fusion(f32[192,8,1024]{2,1,0:T(8,128)S(1)} %bitcast.46, bf16[8,192,1024]{2,1,0:T(8,128)(2,1)S(1)} %copy-done.1), kind=kLoop, calls=%fused_computation.40 | loop fusion | flops 11001856 | bytes 15761408 | tf_op jit(solution)/shard_map/reduce_sum | solution.py:12
  194.9 0.0 copy-start.3
  194.9 0.0 copy-start.4
  194.9 51.1 %psum.14 = f32[8,1024]{1,0:T(8,128)S(1)} all-reduce(f32[8,1024]{1,0:T(8,128)S(1)} %get-tuple-element.5), channel_id=1, replica_groups=mesh['seq'=64,'chan'=4] {'chan'}, use_global_device_ids=true, to_apply=%region_1.0 | all-reduce | flops 8192 | bytes 65536 | tf_op jit(solution)/shard_map/psum | solution.py:12
  246.0 3.7 %multiply_reduce_fusion = f32[8,1024]{1,0:T(8,128)S(1)} fusion(f32[8,192,1024]{2,1,0:T(8,128)} %get-tuple-element.6, f32[8,1024]{1,0:T(8,128)S(1)} %broadcast_multiply_fusion), kind=kLoop, calls=%fused_computation.21 | loop fusion | flops 4710400 | bytes 6356992 | tf_op jit(solution)/shard_map/reduce_sum | solution.py:15
  249.7 16.0 %psum.15 = f32[8,1024]{1,0:T(8,128)S(1)} all-reduce(f32[8,1024]{1,0:T(8,128)S(1)} %multiply_reduce_fusion), channel_id=1, replica_groups=mesh['seq'=64,'chan'=4] {'chan'}, use_global_device_ids=true, to_apply=%region_3.0 | all-reduce | flops 8192 | bytes 65536 | tf_op jit(solution)/shard_map/psum | solution.py:15
  265.7 0.0 copy-done.3
  265.7 0.0 copy-done.4
  265.7 14.8 %fusion.16 = bf16[8,192,1024]{2,1,0:T(8,128)(2,1)} fusion(f32[8,192,1024]{2,1,0:T(8,128)} %get-tuple-element.6, f32[8,1024]{1,0:T(8,128)S(1)} %add_rsqrt_fusion, f32[8,1024]{1,0:T(8,128)S(1)} %broadcast_multiply_fusion, bf16[1,192,768]{2,1,0:T(8,128)(2,1)S(1)} %copy-done.3, bf16[1,192,768]{2,1,0:T(8,128)(2,1)S(1)} %copy-done.4), kind=kOutput, calls=%fused_computation.19 | convolution fusion | flops 4896325632 | bytes 10092544 | tf_op jit(solution)/shard_map/xhy,kh->xky/dot_general | solution.py:20
  (2 shorter events, 0.0 us)
Async XLA Ops:
  0.0 1.6 copy-start
  7.7 93.0 %copy-start.2 = (bf16[512,512]{1,0:T(8,128)(2,1)S(1)}, bf16[512,512]{1,0:T(8,128)(2,1)}, u32[]{:S(2)}) copy-start(bf16[512,512]{1,0:T(8,128)(2,1)} %param.9) | copy-start | bytes 1572868
  184.7 1.9 copy-start.1
  194.9 70.8 %copy-start.3 = (bf16[1,192,768]{2,1,0:T(8,128)(2,1)S(1)}, bf16[1,192,768]{2,1,0:T(8,128)(2,1)}, u32[]{:S(2)}) copy-start(bf16[1,192,768]{2,1,0:T(8,128)(2,1)} %param.11) | copy-start | bytes 884740
  194.9 70.8 %copy-start.4 = (bf16[1,192,768]{2,1,0:T(8,128)(2,1)S(1)}, bf16[1,192,768]{2,1,0:T(8,128)(2,1)}, u32[]{:S(2)}) copy-start(bf16[1,192,768]{2,1,0:T(8,128)(2,1)} %param.10) | copy-start | bytes 884740
where the time goes:
time: 281 us
  blocking collectives  230 us (82%)
  matrix products  24.4 us (9%)
  other arithmetic  13.3 us (5%)
  local copies, waits for them, and re-layouts  13 us (5%)
    all_to_all x1, blocking collectives, body(): lax.all_to_all(by_channel, 'seq', split_axis=0, concat_axis=1, tiled=True)  91.3 us
    all_to_all x1, blocking collectives, body(): lax.all_to_all(mixed.astype(jnp.bfloat16), 'seq', split_axis=1, concat_ax...  71.4 us
    psum x1, blocking collectives, finish(): total = lax.psum(jnp.sum(gated, axis=1), 'chan')  51.1 us
    psum x1, blocking collectives, finish(): spread = lax.psum(jnp.sum(centered * centered, axis=1), 'chan') / D  16 us
    dot_general x1, matrix products, finish(): jnp.einsum('xhy,kh->xky', hidden, down_weight[0], preferred_element_type=...  14.8 us
    reduce_sum x1, other arithmetic, finish(): total = lax.psum(jnp.sum(gated, axis=1), 'chan')  8.29 us
    convert_element_type x1, local copies, waits for them, and re-layouts, body(): mixed.astype(jnp.bfloat16)  7.78 us
    dot_general x1, matrix products, body(): jnp.einsum('rck,bk->rcb', tokens, row_factor, preferred_element_type=jnp....  6.08 us

commit v1 on v0

--- a/solution.py
+++ b/solution.py
@@ -22,10 +22,17 @@
 
 
 def body(tokens, filter_gain, row_factor, col_factor, up_weight, down_weight):
+
+    def press_wall_on(frame_in):
+        return jnp.concatenate(
+            lax.all_to_all(jnp.stack(jnp.split(frame_in, lax.psum(1, "seq"), axis=0)), "seq", 0, 0),
+            axis=1,
+        )
+
     spun = jnp.einsum("rck,bk->rcb", tokens, row_factor, preferred_element_type=jnp.float32)
     filtered = (filter_gain.astype(jnp.float32) * spun).astype(jnp.bfloat16)
     by_channel = jnp.transpose(filtered, (1, 0, 2))
-    owned = lax.all_to_all(by_channel, "seq", split_axis=0, concat_axis=1, tiled=True)
+    owned = press_wall_on(by_channel)
     mixed = jnp.einsum("ak,ckb->cab", col_factor, owned, preferred_element_type=jnp.float32)
     back = lax.all_to_all(
         mixed.astype(jnp.bfloat16), "seq", split_axis=1, concat_axis=0, tiled=True

time: 281 us -> 284 us (1.011)
  local copies, waits for them, and re-layouts: 13 us -> 16.2 us
    unnamed x10 -> x73, local copies, waits for them, and re-layouts: 2.37 us -> 5.49 us
where the time goes in v1:
time: 284 us
  blocking collectives  230 us (81%)
  matrix products  24.4 us (9%)
  local copies, waits for them, and re-layouts  16.2 us (6%)
  other arithmetic  13.3 us (5%)
    all_to_all x1, blocking collectives, press_wall_on(): lax.all_to_all(jnp.stack(jnp.split(frame_in, lax.psum(1, 'seq'), axis=0))...  91.4 us
    all_to_all x1, blocking collectives, body(): lax.all_to_all(mixed.astype(jnp.bfloat16), 'seq', split_axis=1, concat_ax...  71.4 us
    psum x1, blocking collectives, finish(): total = lax.psum(jnp.sum(gated, axis=1), 'chan')  51.1 us
    psum x1, blocking collectives, finish(): spread = lax.psum(jnp.sum(centered * centered, axis=1), 'chan') / D  16 us
    dot_general x1, matrix products, finish(): jnp.einsum('xhy,kh->xky', hidden, down_weight[0], preferred_element_type=...  14.8 us
    reduce_sum x1, other arithmetic, finish(): total = lax.psum(jnp.sum(gated, axis=1), 'chan')  8.29 us
    convert_element_type x1, local copies, waits for them, and re-layouts, body(): mixed.astype(jnp.bfloat16)  7.78 us
    dot_general x1, matrix products, body(): jnp.einsum('rck,bk->rcb', tokens, row_factor, preferred_element_type=jnp....  6.08 us

profile of v1, /device:TPU:2, one launch (start us, length us, event | category | flops | bytes accessed | tf_op | source)
XLA Modules:
  0.0 283.9 jit_solution(4160892861983925364)
XLA Ops:
  0.0 1.6 copy-done
  1.6 6.1 %fusion.17 = bf16[192,8,1024]{2,0,1:T(8,128)(2,1)S(1)} fusion(bf16[8,192,1024]{2,1,0:T(8,128)(2,1)} %param.7, bf16[8,192,1024]{2,1,0:T(8,128)(2,1)} %param.6, bf16[1024,1024]{1,0:T(8,128)(2,1)S(1)} %copy-done), kind=kOutput, calls=%fused_computation.23 | convolution fusion | flops 3225944064 | bytes 11534336 | tf_op jit(solution)/shard_map/rck,bk->rcb/dot_general | solution.py:32
  7.8 0.1 constant_dynamic-update-slice_fusion.61
  7.9 0.1 constant_dynamic-update-slice_fusion.58
  8.2 0.1 constant_dynamic-update-slice_fusion.53
  8.3 0.1 constant_dynamic-update-slice_fusion.50
  8.6 0.1 constant_dynamic-update-slice_fusion.45
  8.7 0.1 constant_dynamic-update-slice_fusion.42
  9.0 0.1 constant_dynamic-update-slice_fusion.37
  9.2 0.1 constant_dynamic-update-slice_fusion.34
  9.4 0.1 constant_dynamic-update-slice_fusion.29
  11.0 1.7 copy.22
  12.7 91.4 %all_to_all.14 = bf16[64,3,8,1024]{3,2,1,0:T(8,128)(2,1)S(1)} all-to-all(bf16[64,3,8,1024]{3,2,1,0:T(8,128)(2,1)S(1)} %copy.22), channel_id=1, replica_groups=mesh['seq'=64,'chan'=4] {'seq'}, dimensions={0} | all-to-all | bytes 6291456 | tf_op jit(solution)/shard_map/all_to_all | solution.py:28
  104.1 3.5 %convert_bitcast_fusion.1 = bf16[3,512,1024]{1,2,0:T(8,128)(2,1)} fusion(bf16[64,3,8,1024]{3,2,1,0:T(8,128)(2,1)S(1)} %all_to_all.14, bf16[512,512]{1,0:T(8,128)(2,1)S(1)} %copy-done.2), kind=kOutput, calls=%fused_computation.29 | convolution fusion | flops 1612185600 | bytes 6815744 | tf_op jit(solution)/shard_map/ak,ckb->cab/dot_general | solution.py:36
  107.6 7.8 %copy.25 = bf16[3,512,1024]{2,0,1:T(4,128)(2,1)} copy(bf16[3,512,1024]{1,2,0:T(8,128)(2,1)} %convert_bitcast_fusion.1) | data formatting | bytes 6291456 | tf_op jit(solution)/shard_map/convert_element_type | solution.py:38
  115.4 71.4 %all_to_all.15 = bf16[3,512,1024]{2,0,1:T(4,128)(2,1)S(1)} all-to-all(bf16[3,512,1024]{2,0,1:T(4,128)(2,1)} %copy.25), channel_id=1, replica_groups=mesh['seq'=64,'chan'=4] {'seq'}, dimensions={1} | all-to-all | bytes 6291456 | tf_op jit(solution)/shard_map/all_to_all | solution.py:37
  186.8 1.4 convert_bitcast_fusion
  188.2 1.1 copy.27
  189.3 0.8 copy-done.1
  190.0 8.3 %fusion.38 = (f32[8,1024]{1,0:T(8,128)S(1)}, f32[8,192,1024]{2,1,0:T(8,128)}) fusion(f32[192,8,1024]{2,1,0:T(8,128)S(1)} %bitcast.301, bf16[8,192,1024]{2,1,0:T(8,128)(2,1)S(1)} %copy-done.1), kind=kLoop, calls=%fused_computation.168 | loop fusion | flops 11001856 | bytes 15761408 | tf_op jit(solution)/shard_map/reduce_sum | solution.py:12
  198.3 51.1 %psum.14 = f32[8,1024]{1,0:T(8,128)S(1)} all-reduce(f32[8,1024]{1,0:T(8,128)S(1)} %get-tuple-element.5), channel_id=1, replica_groups=mesh['seq'=64,'chan'=4] {'chan'}, use_global_device_ids=true, to_apply=%region_1.0 | all-reduce | flops 8192 | bytes 65536 | tf_op jit(solution)/shard_map/psum | solution.py:12
  249.4 3.7 %multiply_reduce_fusion = f32[8,1024]{1,0:T(8,128)S(1)} fusion(f32[8,192,1024]{2,1,0:T(8,128)} %get-tuple-element.6, f32[8,1024]{1,0:T(8,128)S(1)} %broadcast_multiply_fusion), kind=kLoop, calls=%fused_computation.21 | loop fusion | flops 4710400 | bytes 6356992 | tf_op jit(solution)/shard_map/reduce_sum | solution.py:15
  253.1 16.0 %psum.15 = f32[8,1024]{1,0:T(8,128)S(1)} all-reduce(f32[8,1024]{1,0:T(8,128)S(1)} %multiply_reduce_fusion), channel_id=1, replica_groups=mesh['seq'=64,'chan'=4] {'chan'}, use_global_device_ids=true, to_apply=%region_3.0 | all-reduce | flops 8192 | bytes 65536 | tf_op jit(solution)/shard_map/psum | solution.py:15
  269.1 14.8 %fusion.16 = bf16[8,192,1024]{2,1,0:T(8,128)(2,1)} fusion(f32[8,192,1024]{2,1,0:T(8,128)} %get-tuple-element.6, f32[8,1024]{1,0:T(8,128)S(1)} %add_rsqrt_fusion, f32[8,1024]{1,0:T(8,128)S(1)} %broadcast_multiply_fusion, bf16[1,192,768]{2,1,0:T(8,128)(2,1)S(1)} %copy-done.3, bf16[1,192,768]{2,1,0:T(8,128)(2,1)S(1)} %copy-done.4), kind=kOutput, calls=%fused_computation.19 | convolution fusion | flops 4896325632 | bytes 10092544 | tf_op jit(solution)/shard_map/xhy,kh->xky/dot_general | solution.py:20
  (65 shorter events, 2.7 us)
Async XLA Ops:
  0.0 1.6 copy-start
  12.7 91.4 %copy-start.2 = (bf16[512,512]{1,0:T(8,128)(2,1)S(1)}, bf16[512,512]{1,0:T(8,128)(2,1)}, u32[]{:S(2)}) copy-start(bf16[512,512]{1,0:T(8,128)(2,1)} %param.9) | copy-start | bytes 1572868
  188.1 1.9 copy-start.1
  198.3 70.8 %copy-start.3 = (bf16[1,192,768]{2,1,0:T(8,128)(2,1)S(1)}, bf16[1,192,768]{2,1,0:T(8,128)(2,1)}, u32[]{:S(2)}) copy-start(bf16[1,192,768]{2,1,0:T(8,128)(2,1)} %param.11) | copy-start | bytes 884740
  198.3 70.8 %copy-start.4 = (bf16[1,192,768]{2,1,0:T(8,128)(2,1)S(1)}, bf16[1,192,768]{2,1,0:T(8,128)(2,1)}, u32[]{:S(2)}) copy-start(bf16[1,192,768]{2,1,0:T(8,128)(2,1)} %param.10) | copy-start | bytes 884740
